TPU v7x, 512 devices: a whole 4x8x8 slice. The times are simulated.
512 devices in a mesh: row: 64 (over y, x, core), col: 8 (over z).
Axes of the slice: x: 4, y: 8, z: 8, core: 2. Of those that a mesh axis runs over, the one named last changes fastest.
Arguments:
- hamiltonian: float32 [24576, 24576], P('row', 'col'), as said below
- previous: float32 [24576, 56], P('row', 'col'), may hold values from -6 to 6
- correlation_map: int32 [24576], P('row'), may hold values from 0 to 24575, each once
- lower_cut: float32 [1], replicated, may hold values from 0.5 to 1.5
- upper_bound: float32 [1], replicated, may hold values from 5.5 to 6.5
Outputs:
- basis_out: float32 [24576, 56], P('row', 'col')
- ritz_matrix: float32 [56, 56], replicated
Inputs may be any that keep to these rules, and one draw needn't show every extreme that they name: correlation_map names every index of 0 .. 24575 exactly once. hamiltonian is symmetric.
All inputs are finite; a program needn't handle non-finite values.
Results may differ from a plain program's by a relative error of at most 0.00013.
Values sent between devices are 32-bit elements; how exact they have to be, the bound alone decides.
A program may use at most 64 MiB of HBM per device.

v0:
```python
import jax
import jax.numpy as jnp
from jax import lax
from jax.sharding import PartitionSpec as P

N = 24576
DEG = 4


def body(hamiltonian, previous, correlation_map, lower_cut, upper_bound):
    column_groups = lax.axis_size("col")
    group_width = previous.shape[1]
    width = group_width * column_groups
    centre = (upper_bound[0] + lower_cut[0]) * 0.5
    half_width = (upper_bound[0] - lower_cut[0]) * 0.5
    spread = lax.all_gather(previous, "row", axis=0, tiled=True)
    start_block = jnp.take(spread, correlation_map, axis=0)

    def operate_on(vectors):
        spread_rows = lax.all_gather(vectors, "row", axis=0, tiled=True)
        wanted = lax.all_to_all(spread_rows, "col", split_axis=0, concat_axis=1, tiled=True)
        partial_sum = jnp.dot(hamiltonian, wanted, precision=lax.Precision.HIGHEST)
        return lax.psum_scatter(partial_sum, "col", scatter_dimension=1, tiled=True)

    earlier = start_block
    current = (operate_on(earlier) - centre * earlier) / half_width
    for repeat in range(DEG - 1):
        following = 2.0 * (operate_on(current) - centre * current) / half_width - earlier
        earlier = current
        current = following
    column_index = lax.axis_index("col")
    full_rows = lax.all_gather(current, "col", axis=1, tiled=True)
    empty = jnp.zeros((width, width), jnp.float32)
    block_rows = jnp.dot(current.T, full_rows, precision=lax.Precision.HIGHEST)
    gram_part = lax.dynamic_update_slice_in_dim(empty, block_rows, column_index * group_width, 0)
    gram_total = lax.psum(gram_part, ("row", "col"))
    applied = operate_on(current)
    block_cols = jnp.dot(full_rows.T, applied, precision=lax.Precision.HIGHEST)
    proj_total = lax.psum(
        lax.dynamic_update_slice_in_dim(empty, block_cols, column_index * group_width, 1),
        ("row", "col"),
    )
    gram_matrix = gram_total / N
    projected = proj_total / N
    factor = jnp.linalg.cholesky(gram_matrix)
    identity = jnp.eye(width, dtype=jnp.float32)
    inverse = lax.linalg.triangular_solve(factor, identity, left_side=True, lower=True)
    own_columns = lax.dynamic_slice_in_dim(inverse.T, column_index * group_width, group_width, 1)
    basis_out = jnp.dot(full_rows, own_columns, precision=lax.Precision.HIGHEST)
    ritz_matrix = jnp.dot(
        jnp.dot(inverse, projected, precision=lax.Precision.HIGHEST),
        inverse.T,
        precision=lax.Precision.HIGHEST,
    )
    return (basis_out, ritz_matrix)


def solution(mesh):
    return jax.shard_map(
        body,
        mesh=mesh,
        in_specs=(P("row", "col"), P("row", "col"), P("row"), P(), P()),
        out_specs=(P("row", "col"), P()),
        check_vma=False,
    )
```

profile of v0, /device:TPU:1, one launch (start us, length us, event | category | flops | bytes accessed | tf_op | source)
XLA Modules:
  0.0 1014.7 jit_solution(17210025577529272954)
XLA Ops:
  8.6 0.8 copy.41
  9.4 70.1 %all_gather.21 = f32[24576,7]{1,0:T(8,128)} all-gather(f32[384,7]{1,0:T(8,128)S(1)} %copy.41), channel_id=1, replica_groups=mesh['row'=64,'col'=8] {'row'}, dimensions={0}, use_global_device_ids=true | all-gather | bytes 698880 | tf_op jit(solution)/shard_map/all_gather | solution.py:16
  79.6 5.7 gather_fusion
  85.4 48.9 %all_gather.22 = f32[24576,7]{0,1:T(8,128)S(1)} all-gather(f32[384,7]{0,1:T(8,128)S(1)} %broadcast_select_fusion), channel_id=1, replica_groups=mesh['row'=64,'col'=8] {'row'}, dimensions={0}, use_global_device_ids=true | all-gather | bytes 698880 | tf_op jit(solution)/shard_map/all_gather | solution.py:20
  134.3 30.6 %all_to_all.95 = f32[8,3072,7]{1,2,0:T(8,128)S(1)} all-to-all(f32[8,3072,7]{1,2,0:T(8,128)S(1)} %bitcast.63), channel_id=1, replica_groups=mesh['row'=64,'col'=8] {'col'}, dimensions={0} | all-to-all | bytes 1376256 | tf_op jit(solution)/shard_map/all_to_all | solution.py:21
  164.9 7.4 convolution_bitcast_fusion.4
  173.7 1.3 dynamic-slice.4
  175.7 61.5 %all-reduce.12.cloned.1.call-done = f32[384,56]{0,1:T(8,128)} async-done(((f32[384,56]{0,1:T(8,128)}), f32[384,56]{0,1:T(8,128)}) %all-reduce.12.cloned.1.call-update) | async-done | bytes 86032
  237.9 56.2 %all_gather.23 = f32[24576,7]{0,1:T(8,128)S(1)} all-gather(f32[384,7]{0,1:T(8,128)S(1)} %fusion.18), channel_id=1, replica_groups=mesh['row'=64,'col'=8] {'row'}, dimensions={0}, use_global_device_ids=true | all-gather | bytes 698880 | tf_op jit(solution)/shard_map/all_gather | solution.py:20
  294.1 28.4 %all_to_all.96 = f32[8,3072,7]{1,2,0:T(8,128)S(1)} all-to-all(f32[8,3072,7]{1,2,0:T(8,128)S(1)} %bitcast.68), channel_id=1, replica_groups=mesh['row'=64,'col'=8] {'col'}, dimensions={0} | all-to-all | bytes 1376256 | tf_op jit(solution)/shard_map/all_to_all | solution.py:21
  322.6 7.4 convolution_bitcast_fusion.3
  330.1 64.8 %all-reduce.14.cloned.1.call-done = f32[384,56]{0,1:T(8,128)} async-done(((f32[384,56]{0,1:T(8,128)}), f32[384,56]{0,1:T(8,128)}) %all-reduce.14.cloned.1.call-update) | async-done | bytes 86032
  395.6 55.7 %all_gather.24 = f32[24576,7]{0,1:T(8,128)S(1)} all-gather(f32[384,7]{0,1:T(8,128)S(1)} %fusion.17), channel_id=1, replica_groups=mesh['row'=64,'col'=8] {'row'}, dimensions={0}, use_global_device_ids=true | all-gather | bytes 698880 | tf_op jit(solution)/shard_map/all_gather | solution.py:20
  451.4 28.6 %all_to_all.97 = f32[8,3072,7]{1,2,0:T(8,128)S(1)} all-to-all(f32[8,3072,7]{1,2,0:T(8,128)S(1)} %bitcast.69), channel_id=1, replica_groups=mesh['row'=64,'col'=8] {'col'}, dimensions={0} | all-to-all | bytes 1376256 | tf_op jit(solution)/shard_map/all_to_all | solution.py:21
  480.0 7.5 convolution_bitcast_fusion.2
  487.5 64.9 %all-reduce.16.cloned.1.call-done = f32[384,56]{0,1:T(8,128)} async-done(((f32[384,56]{0,1:T(8,128)}), f32[384,56]{0,1:T(8,128)}) %all-reduce.16.cloned.1.call-update) | async-done | bytes 86032
  552.4 0.7 fusion.14
  553.2 55.7 %all_gather.25 = f32[24576,7]{0,1:T(8,128)S(1)} all-gather(f32[384,7]{0,1:T(8,128)S(1)} %fusion.14), channel_id=1, replica_groups=mesh['row'=64,'col'=8] {'row'}, dimensions={0}, use_global_device_ids=true | all-gather | bytes 698880 | tf_op jit(solution)/shard_map/all_gather | solution.py:20
  608.8 28.4 %all_to_all.98 = f32[8,3072,7]{1,2,0:T(8,128)S(1)} all-to-all(f32[8,3072,7]{1,2,0:T(8,128)S(1)} %bitcast.70), channel_id=1, replica_groups=mesh['row'=64,'col'=8] {'col'}, dimensions={0} | all-to-all | bytes 1376256 | tf_op jit(solution)/shard_map/all_to_all | solution.py:21
  637.3 7.5 convolution_bitcast_fusion.1
  644.8 64.9 %all-reduce.18.cloned.1.call-done = f32[384,56]{0,1:T(8,128)} async-done(((f32[384,56]{0,1:T(8,128)}), f32[384,56]{0,1:T(8,128)}) %all-reduce.18.cloned.1.call-update) | async-done | bytes 86032
  710.4 60.3 %all_gather.27 = f32[24576,7]{0,1:T(8,128)} all-gather(f32[384,7]{0,1:T(8,128)S(1)} %fusion.11), channel_id=1, replica_groups=mesh['row'=64,'col'=8] {'row'}, dimensions={0}, use_global_device_ids=true | all-gather | bytes 698880 | tf_op jit(solution)/shard_map/all_gather | solution.py:20
  770.7 5.1 all-to-all-start.4
  775.8 33.0 %all-gather = f32[8,7,384]{2,1,0:T(8,128)S(1)} all-gather(f32[1,7,384]{2,1,0:T(8,128)S(1)} %bitcast.71), channel_id=1, replica_groups=mesh['row'=64,'col'=8] {'col'}, dimensions={0}, use_global_device_ids=true | all-gather | bytes 96768 | tf_op jit(solution)/shard_map/all_gather | solution.py:32
  808.9 7.4 convolution_bitcast_fusion
  816.7 74.4 %all-reduce.20.cloned.1.call-done = f32[384,56]{0,1:T(8,128)} async-done(((f32[384,56]{0,1:T(8,128)}), f32[384,56]{0,1:T(8,128)}) %all-reduce.20.cloned.1.call-update) | async-done | bytes 86032
  891.1 1.0 fusion.7
  892.4 102.7 %all-reduce.5 = (f32[56,56]{1,0:T(8,128)S(1)}, f32[56,56]{1,0:T(8,128)S(1)}) all-reduce(f32[56,56]{1,0:T(8,128)S(1)} %dynamic_update_slice.6, f32[56,56]{1,0:T(8,128)S(1)} %dynamic_update_slice.7), channel_id=1, replica_groups=mesh['row'=64,'col'=8] {'row','col'}, use_global_device_ids=true, to_apply=%region_4.5 | all-reduce | flops 6272 | bytes 50176 | tf_op jit(solution)/shard_map/psum | solution.py:36
  995.2 5.1 cholesky.16
  1001.6 4.3 custom-call.6
  1006.2 0.8 fusion.19
  1007.1 0.8 fusion.25
  (38 shorter events, 7.0 us)
Async XLA Ops:
  7.2 230.0 %all-reduce.12.cloned.1.call-start = ((), (), s32[]{:S(2)}) async-start(), calls=%async_computation.5 | async-start | bytes 172032
  172.4 222.5 %all-reduce.14.cloned.1.call-start = ((), (), s32[]{:S(2)}) async-start(), calls=%async_computation.6 | async-start | bytes 172032
  330.0 222.4 %all-reduce.16.cloned.1.call-start = ((), (), s32[]{:S(2)}) async-start(), calls=%async_computation.7 | async-start | bytes 172032
  487.5 222.2 %all-reduce.18.cloned.1.call-start = ((), (), s32[]{:S(2)}) async-start(), calls=%async_computation.8 | async-start | bytes 172032
  770.7 38.1 %all-to-all-start.4 = ((f32[8,3072,7]{1,2,0:T(8,128)}), f32[8,3072,7]{1,2,0:T(8,128)S(1)}, u32[]{:S(2)}, u32[]{:S(2)}) async-start(f32[8,3072,7]{1,2,0:T(8,128)} %bitcast.19), calls=%async_computation.4 | async-start | bytes 1572864 | tf_op jit(solution)/shard_map/all_to_all | solution.py:21
  775.8 115.3 %all-reduce.20.cloned.1.call-start = ((), (), s32[]{:S(2)}) async-start(), calls=%async_computation.9 | async-start | bytes 172032
Sparse Core Ops, SparseCore 0:
  172.5 64.5 all-reduce.11
  330.2 64.6 all-reduce.13
  487.6 64.7 all-reduce.15
  644.9 64.7 all-reduce.17
  816.5 74.5 all-reduce.19
where the time goes:
time: 1020 us; the launch traced here: 1010 us
  blocking collectives  598 us (59%)
  waiting for transfers between devices  330 us (32%)
  matrix products  40.4 us (4%)
  between operations  16.1 us (2%)
  other arithmetic  15.1 us (1%)
    unnamed x10, waiting for transfers between devices  330 us
    all_gather x5, blocking collectives, operate_on(): spread_rows = lax.all_gather(vectors, 'row', axis=0, tiled=True)  277 us
    all_to_all x4, blocking collectives, operate_on(): lax.all_to_all(spread_rows, 'col', split_axis=0, concat_axis=1, tiled=True)  116 us
    psum x1, blocking collectives, body(): gram_total = lax.psum(gram_part, ('row', 'col'))  103 us
    all_gather x1, blocking collectives, body(): spread = lax.all_gather(previous, 'row', axis=0, tiled=True)  70.1 us
    dot_general x5, matrix products, operate_on(): partial_sum = jnp.dot(hamiltonian, wanted, precision=lax.Precision.HIGHEST)  37.2 us
    all_gather x1, blocking collectives, body(): full_rows = lax.all_gather(current, 'col', axis=1, tiled=True)  33 us
  transfers between devices with their start and end apart: 6, of which 5 were waited for; matrix products, arithmetic and copies ran while one was open for 0% of the time, Pallas kernels for 0%

commit v1 on v0

--- a/solution.py
+++ b/solution.py
@@ -29,7 +29,12 @@
         earlier = current
         current = following
     column_index = lax.axis_index("col")
-    full_rows = lax.all_gather(current, "col", axis=1, tiled=True)
+    ring = [current]
+    for hop in range(7):
+        ring.append(lax.ppermute(ring[-1], "col", [(dev, (dev + 1) % 8) for dev in range(8)]))
+    full_rows = jnp.roll(
+        jnp.concatenate(ring[::-1], axis=1), (lax.axis_index("col") + 1) * ring[0].shape[1], axis=1
+    )
     empty = jnp.zeros((width, width), jnp.float32)
     block_rows = jnp.dot(current.T, full_rows, precision=lax.Precision.HIGHEST)
     gram_part = lax.dynamic_update_slice_in_dim(empty, block_rows, column_index * group_width, 0)

time: 1020 us -> 1050 us (1.029)
  waiting for transfers between devices: 330 us -> 369 us
  blocking collectives: 598 us -> 566 us
  starting transfers between devices: 5.3 us -> 21.1 us
    ppermute x0 -> x7, waiting for transfers between devices: none -> 35 us  [body(): lax.ppermute(ring[-1], 'col', [(dev, (dev + 1) % 8) for dev in range(8)])]
    all_gather x1 -> x0, blocking collectives: 33 us -> none  [body(): full_rows = lax.all_gather(current, 'col', axis=1, tiled=True)]
    ppermute x0 -> x7, starting transfers between devices: none -> 15.8 us  [body(): lax.ppermute(ring[-1], 'col', [(dev, (dev + 1) % 8) for dev in range(8)])]
  transfers between devices with their start and end apart: 6 -> 13, of which waited for: 5 -> 12; matrix products, arithmetic and copies ran while one was open for 0% -> 0% of each run, Pallas kernels for 0% -> 0%
where the time goes in v1:
time: 1050 us; the launch traced here: 1040 us
  blocking collectives  566 us (54%)
  waiting for transfers between devices  369 us (35%)
  matrix products  40.4 us (4%)
  starting transfers between devices  21.1 us (2%)
  between operations  16.2 us (2%)
  other arithmetic  15.1 us (1%)
    unnamed x10, waiting for transfers between devices  334 us
    all_gather x5, blocking collectives, operate_on(): spread_rows = lax.all_gather(vectors, 'row', axis=0, tiled=True)  277 us
    all_to_all x4, blocking collectives, operate_on(): lax.all_to_all(spread_rows, 'col', split_axis=0, concat_axis=1, tiled=True)  116 us
    psum x1, blocking collectives, body(): gram_total = lax.psum(gram_part, ('row', 'col'))  103 us
    all_gather x1, blocking collectives, body(): spread = lax.all_gather(previous, 'row', axis=0, tiled=True)  70.1 us
    dot_general x5, matrix products, operate_on(): partial_sum = jnp.dot(hamiltonian, wanted, precision=lax.Precision.HIGHEST)  37.2 us
    ppermute x7, waiting for transfers between devices, body(): lax.ppermute(ring[-1], 'col', [(dev, (dev + 1) % 8) for dev in range(8)])  35 us
  transfers between devices with their start and end apart: 13, of which 12 were waited for; matrix products, arithmetic and copies ran while one was open for 0% of the time, Pallas kernels for 0%

profile of v1, /device:TPU:1, one launch (start us, length us, event | category | flops | bytes accessed | tf_op | source)
XLA Modules:
  0.0 1037.8 jit_solution(10930689066398907103)
XLA Ops:
  9.4 70.1 %all_gather.18 = f32[24576,7]{1,0:T(8,128)} all-gather(f32[384,7]{1,0:T(8,128)S(1)} %copy.40), channel_id=1, replica_groups=mesh['row'=64,'col'=8] {'row'}, dimensions={0}, use_global_device_ids=true | all-gather | bytes 698880 | tf_op jit(solution)/shard_map/all_gather | solution.py:16
  79.6 5.7 gather_fusion
  85.4 48.9 %all_gather.19 = f32[24576,7]{0,1:T(8,128)S(1)} all-gather(f32[384,7]{0,1:T(8,128)S(1)} %broadcast_select_fusion), channel_id=1, replica_groups=mesh['row'=64,'col'=8] {'row'}, dimensions={0}, use_global_device_ids=true | all-gather | bytes 698880 | tf_op jit(solution)/shard_map/all_gather | solution.py:20
  134.3 30.6 %all_to_all.95 = f32[8,3072,7]{1,2,0:T(8,128)S(1)} all-to-all(f32[8,3072,7]{1,2,0:T(8,128)S(1)} %bitcast.57), channel_id=1, replica_groups=mesh['row'=64,'col'=8] {'col'}, dimensions={0} | all-to-all | bytes 1376256 | tf_op jit(solution)/shard_map/all_to_all | solution.py:21
  164.9 7.4 convolution_bitcast_fusion.4
  175.7 61.5 %all-reduce.12.cloned.1.call-done = f32[384,56]{0,1:T(8,128)} async-done(((f32[384,56]{0,1:T(8,128)}), f32[384,56]{0,1:T(8,128)}) %all-reduce.12.cloned.1.call-update) | async-done | bytes 86032
  237.9 56.2 %all_gather.20 = f32[24576,7]{0,1:T(8,128)S(1)} all-gather(f32[384,7]{0,1:T(8,128)S(1)} %fusion.23), channel_id=1, replica_groups=mesh['row'=64,'col'=8] {'row'}, dimensions={0}, use_global_device_ids=true | all-gather | bytes 698880 | tf_op jit(solution)/shard_map/all_gather | solution.py:20
  294.1 28.4 %all_to_all.96 = f32[8,3072,7]{1,2,0:T(8,128)S(1)} all-to-all(f32[8,3072,7]{1,2,0:T(8,128)S(1)} %bitcast.62), channel_id=1, replica_groups=mesh['row'=64,'col'=8] {'col'}, dimensions={0} | all-to-all | bytes 1376256 | tf_op jit(solution)/shard_map/all_to_all | solution.py:21
  322.6 7.4 convolution_bitcast_fusion.3
  330.1 64.8 %all-reduce.14.cloned.1.call-done = f32[384,56]{0,1:T(8,128)} async-done(((f32[384,56]{0,1:T(8,128)}), f32[384,56]{0,1:T(8,128)}) %all-reduce.14.cloned.1.call-update) | async-done | bytes 86032
  395.6 55.7 %all_gather.21 = f32[24576,7]{0,1:T(8,128)S(1)} all-gather(f32[384,7]{0,1:T(8,128)S(1)} %fusion.22), channel_id=1, replica_groups=mesh['row'=64,'col'=8] {'row'}, dimensions={0}, use_global_device_ids=true | all-gather | bytes 698880 | tf_op jit(solution)/shard_map/all_gather | solution.py:20
  451.3 28.6 %all_to_all.97 = f32[8,3072,7]{1,2,0:T(8,128)S(1)} all-to-all(f32[8,3072,7]{1,2,0:T(8,128)S(1)} %bitcast.63), channel_id=1, replica_groups=mesh['row'=64,'col'=8] {'col'}, dimensions={0} | all-to-all | bytes 1376256 | tf_op jit(solution)/shard_map/all_to_all | solution.py:21
  480.0 7.5 convolution_bitcast_fusion.2
  487.5 64.8 %all-reduce.16.cloned.1.call-done = f32[384,56]{0,1:T(8,128)} async-done(((f32[384,56]{0,1:T(8,128)}), f32[384,56]{0,1:T(8,128)}) %all-reduce.16.cloned.1.call-update) | async-done | bytes 86032
  553.1 55.7 %all_gather.22 = f32[24576,7]{0,1:T(8,128)S(1)} all-gather(f32[384,7]{0,1:T(8,128)S(1)} %fusion.19), channel_id=1, replica_groups=mesh['row'=64,'col'=8] {'row'}, dimensions={0}, use_global_device_ids=true | all-gather | bytes 698880 | tf_op jit(solution)/shard_map/all_gather | solution.py:20
  608.8 28.4 %all_to_all.98 = f32[8,3072,7]{1,2,0:T(8,128)S(1)} all-to-all(f32[8,3072,7]{1,2,0:T(8,128)S(1)} %bitcast.64), channel_id=1, replica_groups=mesh['row'=64,'col'=8] {'col'}, dimensions={0} | all-to-all | bytes 1376256 | tf_op jit(solution)/shard_map/all_to_all | solution.py:21
  637.3 7.4 convolution_bitcast_fusion.1
  644.7 64.8 %all-reduce.18.cloned.1.call-done = f32[384,56]{0,1:T(8,128)} async-done(((f32[384,56]{0,1:T(8,128)}), f32[384,56]{0,1:T(8,128)}) %all-reduce.18.cloned.1.call-update) | async-done | bytes 86032
  710.3 60.6 %all_gather.23 = f32[24576,7]{0,1:T(8,128)} all-gather(f32[384,7]{0,1:T(8,128)S(1)} %fusion.16), channel_id=1, replica_groups=mesh['row'=64,'col'=8] {'row'}, dimensions={0}, use_global_device_ids=true | all-gather | bytes 698880 | tf_op jit(solution)/shard_map/all_gather | solution.py:20
  770.9 5.1 all-to-all-start.4
  779.3 12.8 %collective-permute-done = f32[384,7]{0,1:T(8,128)S(1)} collective-permute-done((f32[384,7]{0,1:T(8,128)S(1)}, f32[384,7]{0,1:T(8,128)S(1)}, u32[]{:S(2)}, u32[]{:S(2)}) %collective-permute-start) | collective-permute-done | bytes 10784 | tf_op jit(solution)/shard_map/ppermute | solution.py:34
  795.0 3.7 collective-permute-done.1
  800.7 3.7 collective-permute-done.2
  806.3 3.7 collective-permute-done.3
  811.9 3.7 collective-permute-done.4
  817.6 3.7 collective-permute-done.5
  823.2 3.7 collective-permute-done.6
  828.2 7.4 convolution_bitcast_fusion
  836.0 78.2 %all-reduce.20.cloned.1.call-done = f32[384,56]{0,1:T(8,128)} async-done(((f32[384,56]{0,1:T(8,128)}), f32[384,56]{0,1:T(8,128)}) %all-reduce.20.cloned.1.call-update) | async-done | bytes 86032
  915.5 102.7 %all-reduce.5 = (f32[56,56]{1,0:T(8,128)S(1)}, f32[56,56]{1,0:T(8,128)S(1)}) all-reduce(f32[56,56]{1,0:T(8,128)S(1)} %dynamic_update_slice.6, f32[56,56]{1,0:T(8,128)S(1)} %dynamic_update_slice.7), channel_id=1, replica_groups=mesh['row'=64,'col'=8] {'row','col'}, use_global_device_ids=true, to_apply=%region_4.5 | all-reduce | flops 6272 | bytes 50176 | tf_op jit(solution)/shard_map/psum | solution.py:41
  1018.2 5.1 cholesky.16
  1024.7 4.3 custom-call.6
  (51 shorter events, 29.3 us)
Async XLA Ops:
  7.2 230.0 %all-reduce.12.cloned.1.call-start = ((), (), s32[]{:S(2)}) async-start(), calls=%async_computation.5 | async-start | bytes 172032
  172.4 222.5 %all-reduce.14.cloned.1.call-start = ((), (), s32[]{:S(2)}) async-start(), calls=%async_computation.6 | async-start | bytes 172032
  330.1 222.3 %all-reduce.16.cloned.1.call-start = ((), (), s32[]{:S(2)}) async-start(), calls=%async_computation.7 | async-start | bytes 172032
  487.5 222.1 %all-reduce.18.cloned.1.call-start = ((), (), s32[]{:S(2)}) async-start(), calls=%async_computation.8 | async-start | bytes 172032
  770.9 57.2 %all-to-all-start.4 = ((f32[8,3072,7]{1,2,0:T(8,128)}), f32[8,3072,7]{1,2,0:T(8,128)S(1)}, u32[]{:S(2)}, u32[]{:S(2)}) async-start(f32[8,3072,7]{1,2,0:T(8,128)} %bitcast.17), calls=%async_computation.4 | async-start | bytes 1572864 | tf_op jit(solution)/shard_map/all_to_all | solution.py:21
  776.0 138.2 %all-reduce.20.cloned.1.call-start = ((), (), s32[]{:S(2)}) async-start(), calls=%async_computation.9 | async-start | bytes 172032
  776.0 16.1 %collective-permute-start = (f32[384,7]{0,1:T(8,128)S(1)}, f32[384,7]{0,1:T(8,128)S(1)}, u32[]{:S(2)}, u32[]{:S(2)}) collective-permute-start(f32[384,7]{0,1:T(8,128)S(1)} %fusion.16), channel_id=1, source_target_pairs={{0,1},{1,2},{2,3},{3,4},{4,5},{5,6},{6,7},{7,0},{8,9},{9,10},{10,1... | collective-permute-start | bytes 32264 | tf_op jit(solution)/shard_map/ppermute | solution.py:34
  792.1 6.6 collective-permute-start.1
  798.7 5.6 collective-permute-start.2
  804.4 5.6 collective-permute-start.3
  810.0 5.6 collective-permute-start.4
  815.6 5.6 collective-permute-start.5
  821.3 5.6 collective-permute-start.6
Sparse Core Ops, SparseCore 0:
  172.5 64.5 all-reduce.11
  330.2 64.6 all-reduce.13
  487.6 64.7 all-reduce.15
  644.9 64.6 all-reduce.17
  835.8 78.3 all-reduce.19
